TPU v7x, 32 devices: a whole 2x2x4 slice. The times are simulated.
32 devices in a mesh: rows: 8 (over y, x, core), loop: 4 (over z).
Axes of the slice: x: 2, y: 2, z: 4, core: 2. Of those that a mesh axis runs over, the one named last changes fastest.
Arguments:
- integrals: float32 [2, 2, 8192, 8192], P(None, None, 'rows', 'loop'), may hold values from -6 to 6
- mask: int32 [2, 64, 64], P(None, 'rows', 'loop'), may hold values 0 or 1
- coeffs: float32 [8192, 640], P('loop'), may hold values from -0.0625 to 0.0625
Outputs:
- exchange: float32 [8192, 8192], P('rows', 'loop')
All inputs are finite; a program needn't handle non-finite values. No bound on the sum of `mask` on one device may be relied on, other than what follows from the above.
Results may differ from a plain program's by a relative error of at most 0.00009.
Values sent between devices are 32-bit elements; how exact they have to be, the bound alone decides.
A program may use at most 192 MiB of HBM per device.

v0:
```python
import jax
import jax.numpy as jnp
from jax import lax
from jax.sharding import PartitionSpec as P

TILE = 128


def local(integrals, mask, coeffs):
    nslab, naux, mrows, lcols = integrals.shape
    blocks = mask.astype(jnp.float32)[:, None, :, None, :, None]
    shaped = integrals.reshape(nslab, naux, mrows // TILE, TILE, lcols // TILE, TILE)
    masked = (shaped * blocks).reshape(nslab * naux, mrows, lcols)
    norbit = coeffs.shape[1]
    loops = lax.axis_size("loop")
    row_count = lax.axis_size("rows")
    mine = norbit // loops
    ratio = row_count // loops
    depth = norbit * nslab * naux
    row_full = lax.psum(
        jnp.einsum("pml,li->ipm", masked, coeffs, precision=lax.Precision.HIGHEST), "loop"
    )
    own_orbits = lax.dynamic_slice_in_dim(row_full, lax.axis_index("loop") * mine, mine, 0)
    row_flat = row_full.reshape(depth, mrows)
    sub_rows = mrows // row_count
    split_rows = own_orbits.reshape(mine, nslab * naux, row_count, sub_rows)
    routed = lax.all_to_all(
        lax.all_to_all(split_rows, "rows", split_axis=2, concat_axis=2, tiled=True),
        "loop",
        split_axis=2,
        concat_axis=0,
        tiled=True,
    )
    piece = lax.all_gather(routed, "rows", axis=3, tiled=True)
    flat = piece.reshape(depth, ratio, piece.shape[3])
    tiles = jnp.einsum("dm,doc->moc", row_flat, flat, precision=lax.Precision.HIGHEST)
    total = tiles.reshape(mrows, lcols)
    scale = 1.0 / jnp.sqrt(jnp.float32(depth))
    return total * scale


def solution(mesh):
    in_specs = (P(None, None, "rows", "loop"), P(None, "rows", "loop"), P("loop", None))
    out_specs = P("rows", "loop")
    return jax.shard_map(local, mesh=mesh, in_specs=in_specs, out_specs=out_specs, check_vma=False)
```

profile of v0, /device:TPU:5, one launch (start us, length us, event | category | flops | bytes accessed | tf_op | source)
XLA Modules:
  0.0 879.5 jit_solution(2462211604459332383)
XLA Ops:
  6.5 0.0 all-reduce.2.cloned.1.call-start
  6.5 0.7 convert_element_type.3
  7.2 11.0 %mul.20 = f32[2,2,8,128,16,128]{5,4,3,2,1,0:T(8,128)} broadcast(f32[2,8,16]{2,1,0:T(8,128)S(1)} %convert_element_type.3), dimensions={0,2,4} | broadcast | bytes 33555456 | tf_op jit(solution)/shard_map/mul | solution.py:13
  18.3 35.5 %mul.21 = f32[4,1024,2048]{2,1,0:T(8,128)} reshape(f32[2,2,8,128,16,128]{5,4,3,2,1,0:T(8,128)} %mul.20) | data formatting | bytes 67108864 | tf_op jit(solution)/shard_map/mul | solution.py:13
  53.7 32.9 %bitcast_multiply_fusion = f32[4,1024,2048]{2,1,0:T(8,128)} fusion(f32[4,1024,2048]{2,1,0:T(8,128)} %mul.21, f32[2,2,1024,2048]{3,2,1,0:T(8,128)} %param.3), kind=kLoop, calls=%fused_computation | loop fusion | flops 8388608 | bytes 100663296 | tf_op jit(solution)/shard_map/mul | solution.py:13
  86.6 87.8 %fusion.2 = f32[640,4,1024]{0,2,1:T(8,128)} fusion(f32[4,1024,2048]{2,1,0:T(8,128)} %bitcast_multiply_fusion, f32[2048,640]{1,0:T(8,128)} %param.5), kind=kOutput, calls=%fused_computation.4 | convolution fusion | flops 64424509440 | bytes 49283072 | tf_op jit(solution)/shard_map/pml,li->ipm/dot_general | solution.py:21
  174.4 0.0 all-reduce.2.cloned.1.call-update
  174.5 0.2 all-gather.2.cloned.1.call-start
  174.7 359.4 %all-reduce.2.cloned.1.call-done = f32[640,4,1024]{0,2,1:T(8,128)} async-done(((f32[640,4,1024]{0,2,1:T(8,128)}), f32[640,4,1024]{0,2,1:T(8,128)}) %all-reduce.2.cloned.1.call-update) | async-done | bytes 10485776 | tf_op jit(solution)/shard_map/psum | solution.py:20
  534.1 5.9 constant_dynamic-slice_fusion
  540.1 4.1 copy.15
  544.2 34.3 %all_to_all.23 = f32[160,4,8,128]{3,0,1,2:T(8,128)S(1)} all-to-all(f32[160,4,8,128]{3,0,1,2:T(8,128)S(1)} %copy.15), channel_id=1, replica_groups=mesh['rows'=8,'loop'=4] {'rows'}, dimensions={2} | all-to-all | bytes 5242880 | tf_op jit(solution)/shard_map/all_to_all | solution.py:28
  578.5 60.9 %all_to_all.24 = f32[160,4,8,128]{3,0,1,2:T(8,128)S(1)} all-to-all(f32[160,4,8,128]{3,0,1,2:T(8,128)S(1)} %all_to_all.23), channel_id=1, replica_groups=mesh['rows'=8,'loop'=4] {'loop'}, dimensions={2} | all-to-all | bytes 5242880 | tf_op jit(solution)/shard_map/all_to_all | solution.py:27
  639.4 1.7 copy.17
  641.1 0.0 all-gather.2.cloned.1.call-update
  641.1 13.2 %copy.13 = f32[640,4,1024]{2,1,0:T(4,128)} copy(f32[640,4,1024]{0,2,1:T(8,128)} %all-reduce.2.cloned.1.call-done) | data formatting | bytes 20971520 | tf_op jit(solution)/shard_map/psum | solution.py:20
  654.3 12.4 %reshape.19 = f32[2560,1024]{1,0:T(8,128)} reshape(f32[640,4,1024]{2,1,0:T(4,128)} %copy.13) | data formatting | bytes 20971520 | tf_op jit(solution)/shard_map/reshape | solution.py:24
  666.7 85.5 %all-gather.2.cloned.1.call-done = f32[640,4,2,1024]{3,0,2,1:T(8,128)} async-done(((f32[640,4,2,128]{3,0,2,1:T(8,128)}), f32[640,4,2,1024]{3,0,2,1:T(8,128)}) %all-gather.2.cloned.1.call-update) | async-done | bytes 20971536 | tf_op jit(solution)/shard_map/all_gather | solution.py:34
  752.2 34.2 %copy.18 = f32[640,4,2,1024]{3,2,1,0:T(2,128)S(1)} copy(f32[640,4,2,1024]{3,0,2,1:T(8,128)} %all-gather.2.cloned.1.call-done) | data formatting | bytes 41943040 | tf_op jit(solution)/shard_map/all_gather | solution.py:34
  786.4 13.6 %copy.22 = f32[320,8,2,1024]{3,1,2,0:T(8,128)} copy(f32[320,8,2,1024]{3,2,1,0:T(2,128)S(1)} %bitcast.26) | data formatting | bytes 41943040
  800.0 72.6 %convolution_multiply_fusion = f32[1024,2048]{1,0:T(8,128)} fusion(f32[2560,1024]{1,0:T(8,128)} %reshape.19, f32[2048,2560]{0,1:T(8,128)} %bitcast.27), kind=kOutput, calls=%fused_computation.3 | convolution fusion | flops 64426606592 | bytes 39845888 | tf_op jit(solution)/shard_map/dm,doc->moc/dot_general | solution.py:36
Async XLA Ops:
  6.5 527.6 %all-reduce.2.cloned.1.call-start = ((), (), s32[]{:S(2)}) async-start(), calls=%async_computation.2 | async-start | bytes 20971520 | tf_op jit(solution)/shard_map/psum | solution.py:20
  174.5 577.7 %all-gather.2.cloned.1.call-start = ((), (), s32[]{:S(2)}) async-start(), calls=%async_computation.3 | async-start | bytes 23592960 | tf_op jit(solution)/shard_map/all_gather | solution.py:34
Sparse Core Ops, SparseCore 0:
  174.6 359.4 all-reduce.1
  641.3 110.8 all-gather.1
where the time goes:
time: 883 us; the launch traced here: 879 us
  waiting for transfers between devices  445 us (50%)
  matrix products  160 us (18%)
  local copies, waits for them, and re-layouts  132 us (15%)
  blocking collectives  95.3 us (11%)
  other arithmetic  33.6 us (4%)
  between operations  13.4 us (2%)
    psum x1, waiting for transfers between devices, local(): lax.psum(jnp.einsum('pml,li->ipm', masked, coeffs, precision=lax.Precisio...  359 us
    dot_general x1, matrix products, local(): jnp.einsum('pml,li->ipm', masked, coeffs, precision=lax.Precision.HIGHEST)  87.8 us
    all_gather x1, waiting for transfers between devices, local(): piece = lax.all_gather(routed, 'rows', axis=3, tiled=True)  85.5 us
    dot_general x1, matrix products, local(): jnp.einsum('dm,doc->moc', row_flat, flat, precision=lax.Precision.HIGHEST)  72.6 us
    all_to_all x1, blocking collectives, local(): lax.all_to_all(lax.all_to_all(split_rows, 'rows', split_axis=2, concat_ax...  60.9 us
    mul x2, local copies, waits for them, and re-layouts, local(): masked = (shaped * blocks).reshape(nslab * naux, mrows, lcols)  46.5 us
    all_to_all x1, blocking collectives, local(): lax.all_to_all(split_rows, 'rows', split_axis=2, concat_axis=2, tiled=True)  34.3 us
    all_gather x1, local copies, waits for them, and re-layouts, local(): piece = lax.all_gather(routed, 'rows', axis=3, tiled=True)  34.2 us
  transfers between devices with their start and end apart: 2, of which 2 were waited for; matrix products, arithmetic and copies ran while one was open for 3% of the time, Pallas kernels for 0%

commit v1 on v0

v1 whole, which is shorter than its diff:
```python
import functools

import jax
import jax.numpy as jnp
from jax import lax
from jax.experimental import pallas as pl
from jax.experimental.pallas import tpu as pltpu
from jax.sharding import PartitionSpec as P

TILE = 128
CHUNK = 32
GROUP = 8
HOP = 2
REACH = 2
SLOTS = 8
MESH = pl.DeviceIdType.MESH


def split(x):
    high = x.astype(jnp.bfloat16)
    low = (x - high.astype(jnp.float32)).astype(jnp.bfloat16)
    return high, low


def half_kernel(integrals_ref, mask_ref, high_ref, low_ref, out_ref):
    rows, cols = integrals_ref.shape[2:]
    blocks = integrals_ref[0, 0].reshape(rows // TILE, TILE, cols)
    high, low = split((blocks * mask_ref[0]).reshape(rows, cols))

    def times(a, b):
        return lax.dot_general(
            a, b, (((1,), (1,)), ((), ())), preferred_element_type=jnp.float32
        )

    out_ref[0] = times(high_ref[...], high) + times(high_ref[...], low) + times(low_ref[...], high)


def half_partial(integrals, mask, coeffs):
    nslab, naux, mrows, lcols = integrals.shape
    norbit = coeffs.shape[1]
    turned = coeffs.T
    rounded = lax.reduce_precision(turned, 8, 7)
    high, low = rounded.astype(jnp.bfloat16), (turned - rounded).astype(jnp.bfloat16)
    blocks = jnp.repeat(mask.astype(jnp.float32), TILE, axis=2)[:, :, None, :]
    tm = 256
    out = pl.pallas_call(
        half_kernel,
        grid=(nslab, naux, mrows // tm),
        out_shape=jax.ShapeDtypeStruct((nslab * naux, norbit, mrows), jnp.float32),
        in_specs=[
            pl.BlockSpec((1, 1, tm, lcols), lambda s, a, m: (s, a, m, 0)),
            pl.BlockSpec((1, tm // TILE, 1, lcols), lambda s, a, m: (s, m, 0, 0)),
            pl.BlockSpec((norbit, lcols), lambda s, a, m: (0, 0)),
            pl.BlockSpec((norbit, lcols), lambda s, a, m: (0, 0)),
        ],
        out_specs=pl.BlockSpec((1, norbit, tm), lambda s, a, m: (s * naux + a, 0, m)),
        name="half",
    )(integrals, blocks, high, low)
    return out.reshape(nslab * naux * norbit, mrows)


def ring_place(pair, pairs):
    if pairs == 4:
        return pair + (pair // 2) * (1 - 2 * lax.rem(pair, 2))
    return pair


def exchange_kernel(
    loops, row_count, scale, part_ref, out_ref, own, pin, sin, cols, left,
    own_sem, up_send, up_recv, dn_send, dn_recv, ch_send, ch_recv, pt_send, pt_recv,
):
    depth, mrows = own.shape
    count = depth // CHUNK
    span = CHUNK * GROUP
    pairs = row_count // 2
    r, l = lax.axis_index("rows"), lax.axis_index("loop")
    pair, core = r // 2, lax.rem(r, 2)
    partner = r + 1 - 2 * core
    turn = 1 - 2 * core
    place = ring_place(pair, pairs)
    far = lax.rem((place - ring_place(l, pairs)) * turn + pairs, pairs)
    ahead = ring_place(lax.rem(place + turn + pairs, pairs), pairs) * 2 + core
    behind = ring_place(lax.rem(place - turn + pairs, pairs), pairs) * 2 + core

    load = pltpu.make_async_copy(part_ref, own, own_sem)
    load.start()

    barrier = pltpu.get_barrier_semaphore()
    for other in (partner, ahead, behind):
        pl.semaphore_signal(barrier, inc=1, device_id={"rows": other}, device_id_type=MESH)

    @pl.when(l > 0)
    def _():
        pl.semaphore_signal(barrier, inc=1, device_id={"loop": l - 1}, device_id_type=MESH)

    @pl.when(l < loops - 1)
    def _():
        pl.semaphore_signal(barrier, inc=1, device_id={"loop": l + 1}, device_id_type=MESH)

    neighbours = jnp.where(l > 0, 1, 0) + jnp.where(l < loops - 1, 1, 0)
    pl.semaphore_wait(barrier, 3 + neighbours)

    load.wait()

    def rows_of(j):
        return pl.ds(pl.multiple_of(j * CHUNK, CHUNK), CHUNK)

    def copy(src, dst, send, recv, j, target):
        return pltpu.make_async_remote_copy(
            src_ref=src, dst_ref=dst, send_sem=send.at[lax.rem(j, SLOTS)], recv_sem=recv.at[j],
            device_id=target, device_id_type=MESH,
        )

    def up(j):
        return copy(pin.at[rows_of(j)], pin.at[rows_of(j)], up_send, up_recv, j, {"loop": l + 1})

    def down(j):
        return copy(sin.at[rows_of(j)], sin.at[rows_of(j)], dn_send, dn_recv, j, {"loop": l - 1})

    def chain(j):
        ref = cols.at[core, rows_of(j)]
        return copy(ref, ref, ch_send, ch_recv, j, {"rows": ahead})

    def share(j):
        ref = cols.at[core, rows_of(j)]
        return copy(ref, ref, pt_send, pt_recv, j, {"rows": partner})

    def taken(j):
        ref = cols.at[1 - core, rows_of(j)]
        return copy(ref, ref, pt_send, pt_recv, j, {"rows": partner})

    def send(make, j):
        @pl.when(j >= SLOTS)
        def _():
            make(j - SLOTS).wait_send()

        make(j).start()

    def line(held, make, j, first, last):
        @pl.when((j >= 0) & (j < count))
        def _():
            at = rows_of(j)

            @pl.when(first)
            def _():
                held[at, :] = own[at, :]

            @pl.when(jnp.logical_not(first))
            def _():
                make(j).wait_recv()
                held[at, :] = held[at, :] + own[at, :]

            @pl.when(jnp.logical_not(last))
            def _():
                send(make, j)

    settle = HOP * jnp.maximum(l, loops - 1 - l)

    def multiply(g):
        at = pl.ds(pl.multiple_of(g * span, span), span)

        @pl.loop(0, mrows // 256)
        def _(m):
            mine = pl.ds(pl.multiple_of(m * 256, 256), 256)
            high, low = split(own[at, mine].T)
            left[mine, pl.ds(0, span)] = high
            left[mine, pl.ds(span, span)] = high
            left[mine, pl.ds(2 * span, span)] = low

        for block in range(2):

            @pl.loop(0, mrows // 256)
            def _(n):
                high, low = split(cols[block, at, pl.ds(pl.multiple_of(n * 256, 256), 256)])
                right = jnp.concatenate([high, low, high], axis=0)
                theirs = pl.ds(pl.multiple_of(block * mrows + n * 256, 256), 256)

                @pl.loop(0, mrows // 256)
                def _(m):
                    mine = pl.ds(pl.multiple_of(m * 256, 256), 256)
                    part = jnp.dot(left[mine, :], right, preferred_element_type=jnp.float32) * scale

                    @pl.when(g == 0)
                    def _():
                        out_ref[mine, theirs] = part

                    @pl.when(g > 0)
                    def _():
                        out_ref[mine, theirs] = out_ref[mine, theirs] + part

    def step(t, carry):
        line(pin, up, t - HOP * l, l == 0, l == loops - 1)
        line(sin, down, t - HOP * (loops - 1 - l), l == loops - 1, l == 0)

        done = t - settle

        @pl.when((done >= 0) & (done < count))
        def _():
            at = rows_of(done)
            total = pin[at, :] + (sin[at, :] - own[at, :])
            own[at, :] = total

            @pl.when(far == 0)
            def _():
                cols[core, at, :] = total

        passed = done - REACH * far

        @pl.when((passed >= 0) & (passed < count))
        def _():
            @pl.when(far > 0)
            def _():
                chain(passed).wait_recv()

            @pl.when(far < pairs - 1)
            def _():
                send(chain, passed)

            send(share, passed)

        ready = done - REACH * pairs

        @pl.when((ready >= 0) & (ready < count))
        def _():
            taken(ready).wait_recv()

            @pl.when(lax.rem(ready, GROUP) == GROUP - 1)
            def _():
                multiply(ready // GROUP)

        return carry

    lax.fori_loop(0, count + HOP * (loops - 1) + REACH * pairs, step, 0)

    def drain(i, carry):
        j = count - SLOTS + i

        @pl.when(l < loops - 1)
        def _():
            up(j).wait_send()

        @pl.when(l > 0)
        def _():
            down(j).wait_send()

        @pl.when(far < pairs - 1)
        def _():
            chain(j).wait_send()

        share(j).wait_send()
        return carry

    lax.fori_loop(0, SLOTS, drain, 0)


def local(loops, row_count, integrals, mask, coeffs):
    mrows, lcols = integrals.shape[2:]
    part = half_partial(integrals, mask, coeffs)
    depth = part.shape[0]
    assert lcols == 2 * mrows and row_count == 2 * loops
    count = depth // CHUNK
    assert depth % (CHUNK * GROUP) == 0
    dma = pltpu.SemaphoreType.DMA
    return pl.pallas_call(
        functools.partial(exchange_kernel, loops, row_count, float(depth) ** -0.5),
        out_shape=jax.ShapeDtypeStruct((mrows, lcols), jnp.float32),
        in_specs=[pl.BlockSpec(memory_space=pl.ANY)],
        out_specs=pl.BlockSpec(memory_space=pltpu.VMEM),
        scratch_shapes=[
            pltpu.VMEM((depth, mrows), jnp.float32),
            pltpu.VMEM((depth, mrows), jnp.float32),
            pltpu.VMEM((depth, mrows), jnp.float32),
            pltpu.VMEM((2, depth, mrows), jnp.float32),
            pltpu.VMEM((mrows, 3 * CHUNK * GROUP), jnp.bfloat16),
            dma,
        ]
        + [dma((SLOTS,)), dma((count,))] * 4,
        compiler_params=pltpu.CompilerParams(
            collective_id=0, has_side_effects=True, vmem_limit_bytes=67043328
        ),
        name="exchange",
    )(part)


def solution(mesh):
    in_specs = (P(None, None, "rows", "loop"), P(None, "rows", "loop"), P("loop", None))
    out_specs = P("rows", "loop")
    body = functools.partial(local, mesh.shape["loop"], mesh.shape["rows"])
    return jax.shard_map(body, mesh=mesh, in_specs=in_specs, out_specs=out_specs, check_vma=False)
```

time: 883 us -> 399 us (0.45)
  waiting for transfers between devices: 445 us -> 0 us
  Pallas kernels: 0 us -> 378 us
  matrix products: 160 us -> 0 us
  local copies, waits for them, and re-layouts: 132 us -> 14.5 us
  blocking collectives: 95.3 us -> 0 us
  other arithmetic: 33.6 us -> 6.62 us
  between operations: 13.4 us -> 0.01 us
    pallas_call x0 -> x2, Pallas kernels: none -> 378 us  [the longest x1 337 us: local(): pl.pallas_call(functools.partial(exchange_kernel, loops, row_count, float...]
    psum x1 -> x0, waiting for transfers between devices: 359 us -> none  [local(): lax.psum(jnp.einsum('pml,li->ipm', masked, coeffs, precision=lax.Precisio...]
    dot_general x2 -> x0, matrix products: 160 us -> none  [the longest x1 87.8 us: local(): jnp.einsum('pml,li->ipm', masked, coeffs, precision=lax.Precision.HIGHEST)]
    all_to_all x2 -> x0, blocking collectives: 95.3 us -> none  [the longest x1 60.9 us: local(): lax.all_to_all(lax.all_to_all(split_rows, 'rows', split_axis=2, concat_ax...]
    all_gather x1 -> x0, waiting for transfers between devices: 85.5 us -> none  [local(): piece = lax.all_gather(routed, 'rows', axis=3, tiled=True)]
    mul x2 -> x0, local copies, waits for them, and re-layouts: 46.5 us -> none  [local(): masked = (shaped * blocks).reshape(nslab * naux, mrows, lcols)]
    all_gather x1 -> x0, local copies, waits for them, and re-layouts: 34.2 us -> none  [local(): piece = lax.all_gather(routed, 'rows', axis=3, tiled=True)]
    mul x1 -> x0, other arithmetic: 32.9 us -> none  [local(): masked = (shaped * blocks).reshape(nslab * naux, mrows, lcols)]
  transfers between devices with their start and end apart: 2 -> 0, of which waited for: 2 -> 0; matrix products, arithmetic and copies ran while one was open for 3% -> 0% of each run, Pallas kernels for 0% -> 0%
where the time goes in v1:
time: 399 us
  Pallas kernels  378 us (95%)
  local copies, waits for them, and re-layouts  14.5 us (4%)
  other arithmetic  6.62 us (2%)
    pallas_call x1, Pallas kernels, local(): pl.pallas_call(functools.partial(exchange_kernel, loops, row_count, float...  337 us
    pallas_call x1, Pallas kernels, half_partial(): pl.pallas_call(half_kernel, grid=(nslab, naux, mrows // tm), out_shape=ja...  40.6 us
    unnamed x2, local copies, waits for them, and re-layouts  13.8 us

profile of v1, /device:TPU:5, one launch (start us, length us, event | category | flops | bytes accessed | tf_op | source)
XLA Modules:
  0.0 399.0 jit_solution(2473629465817730256)
XLA Ops:
  0.0 0.7 convert_element_type.9
  0.7 0.8 broadcast_in_dim.3
  1.5 5.9 %copy.4 = f32[2048,640]{0,1:T(8,128)} copy(f32[2048,640]{1,0:T(8,128)} %param.5) | data formatting | bytes 10485760 | tf_op args[2]
  7.3 5.9 %fusion = (bf16[640,2048]{1,0:T(8,128)(2,1)}, bf16[640,2048]{1,0:T(8,128)(2,1)}) fusion(f32[2048,640]{0,1:T(8,128)} %copy.4), kind=kLoop, calls=%fused_computation.2 | loop fusion | flops 5242880 | bytes 10485760 | tf_op jit(solution)/shard_map/convert_element_type | solution.py:43
  13.3 40.6 %half.1 = f32[4,640,1024]{2,1,0:T(8,128)} custom-call(f32[2,2,1024,2048]{3,2,1,0:T(8,128)} %integrals_ref.1, f32[2,8,1,2048]{3,2,1,0:T(1,128)} %bitcast.6, bf16[640,2048]{1,0:T(8,128)(2,1)} %get-tuple-element.6.high_ref, bf16[640,2048]{1,0:T(8,128)(2,1)} %get-tuple-element.5.low_ref), custom_call_target="tpu_custom_call" | custom-call | tf_op jit(solution)/shard_map/half/pallas_call | solution.py:46
  53.9 337.3 %exchange.1 = f32[1024,2048]{1,0:T(8,128)} custom-call(f32[2560,1024]{1,0:T(8,128)} %bitcast.5), custom_call_target="tpu_custom_call" | custom-call | tf_op jit(solution)/shard_map/exchange/pallas_call | solution.py:264
  391.1 7.9 %copy.6 = f32[1024,2048]{1,0:T(8,128)} copy(f32[1024,2048]{1,0:T(8,128)} %exchange.1) | data formatting | bytes 16777216

commit v2 on v1

v2 whole, which is shorter than its diff:
```python
import functools

import jax
import jax.numpy as jnp
from jax import lax
from jax.experimental import pallas as pl
from jax.experimental.pallas import tpu as pltpu
from jax.sharding import PartitionSpec as P

TILE = 128
CHUNK = 32
GROUP = 8
HOP = 2
REACH = 2
SLOTS = 8
MESH = pl.DeviceIdType.MESH


def split(x):
    high = x.astype(jnp.bfloat16)
    low = (x - high.astype(jnp.float32)).astype(jnp.bfloat16)
    return high, low


def ring_place(pair, pairs):
    if pairs == 4:
        return pair + (pair // 2) * (1 - 2 * lax.rem(pair, 2))
    return pair


def exchange_kernel(
    loops, row_count, scale, integrals_ref, mask_ref, coeffs_ref, out_ref,
    own, pin, sin, cols, left, high_ref, low_ref, tile, spare, tile_sem, coeffs_sem,
    up_send, up_recv, dn_send, dn_recv, ch_send, ch_recv, pt_send, pt_recv,
):
    depth, mrows = own.shape
    naux, lcols = integrals_ref.shape[1], integrals_ref.shape[3]
    norbit = coeffs_ref.shape[1]
    ring = pin.shape[0] // CHUNK
    wide = tile.shape[1]
    tiles = mrows // wide
    tile_count = integrals_ref.shape[0] * naux * tiles
    count = depth // CHUNK
    span = CHUNK * GROUP
    pairs = row_count // 2
    r, l = lax.axis_index("rows"), lax.axis_index("loop")
    pair, core = r // 2, lax.rem(r, 2)
    partner = r + 1 - 2 * core
    turn = 1 - 2 * core
    place = ring_place(pair, pairs)
    far = lax.rem((place - ring_place(l, pairs)) * turn + pairs, pairs)
    ahead = ring_place(lax.rem(place + turn + pairs, pairs), pairs) * 2 + core
    behind = ring_place(lax.rem(place - turn + pairs, pairs), pairs) * 2 + core

    def fetch(u):
        part, m = u // tiles, lax.rem(u, tiles)
        return pltpu.make_async_copy(
            integrals_ref.at[
                part // naux, lax.rem(part, naux), pl.ds(pl.multiple_of(m * wide, wide), wide), :
            ],
            tile.at[lax.rem(u, 2)],
            tile_sem.at[lax.rem(u, 2)],
        )

    def half(u):
        part, m = u // tiles, lax.rem(u, tiles)
        fetch(u).wait()
        blocks = tile[lax.rem(u, 2)].reshape(wide // TILE, TILE, lcols)
        mask = mask_ref[part // naux, m][:, None, :]
        high, low = split((blocks * mask).reshape(wide, lcols))

        def times(a, b):
            return lax.dot_general(
                a, b, (((1,), (1,)), ((), ())), preferred_element_type=jnp.float32
            )

        value = times(high_ref[...], high) + times(high_ref[...], low) + times(low_ref[...], high)
        at = pl.ds(pl.multiple_of(part * norbit, norbit), norbit)
        own[at, pl.ds(pl.multiple_of(m * wide, wide), wide)] = value

        @pl.when(u + 2 < tile_count)
        def _():
            fetch(u + 2).start()

    room = spare if spare.shape == coeffs_ref.shape else cols.at[0, pl.ds(0, lcols), pl.ds(0, norbit)]
    load = pltpu.make_async_copy(coeffs_ref, room, coeffs_sem)
    load.start()
    fetch(0).start()
    fetch(1).start()
    load.wait()

    @pl.loop(0, lcols // 256)
    def _(n):
        at = pl.ds(pl.multiple_of(n * 256, 256), 256)
        high_ref[:, at], low_ref[:, at] = split(room[at, :].T)

    barrier = pltpu.get_barrier_semaphore()
    for other in (partner, ahead, behind):
        pl.semaphore_signal(barrier, inc=1, device_id={"rows": other}, device_id_type=MESH)

    @pl.when(l > 0)
    def _():
        pl.semaphore_signal(barrier, inc=1, device_id={"loop": l - 1}, device_id_type=MESH)

    @pl.when(l < loops - 1)
    def _():
        pl.semaphore_signal(barrier, inc=1, device_id={"loop": l + 1}, device_id_type=MESH)

    neighbours = jnp.where(l > 0, 1, 0) + jnp.where(l < loops - 1, 1, 0)
    pl.semaphore_wait(barrier, 3 + neighbours)

    @pl.loop(0, tiles)
    def _(u):
        half(u)

    pace = max(norbit // CHUNK // tiles, 1)

    def rows_of(j):
        return pl.ds(pl.multiple_of(j * CHUNK, CHUNK), CHUNK)

    def slot_of(j):
        return pl.ds(pl.multiple_of(lax.rem(j, ring) * CHUNK, CHUNK), CHUNK)

    def copy(src, dst, send, recv, j, target):
        return pltpu.make_async_remote_copy(
            src_ref=src, dst_ref=dst, send_sem=send.at[lax.rem(j, SLOTS)], recv_sem=recv.at[j],
            device_id=target, device_id_type=MESH,
        )

    def up(j):
        return copy(pin.at[slot_of(j)], pin.at[slot_of(j)], up_send, up_recv, j, {"loop": l + 1})

    def down(j):
        return copy(sin.at[slot_of(j)], sin.at[slot_of(j)], dn_send, dn_recv, j, {"loop": l - 1})

    def chain(j):
        ref = cols.at[core, rows_of(j)]
        return copy(ref, ref, ch_send, ch_recv, j, {"rows": ahead})

    def share(j):
        ref = cols.at[core, rows_of(j)]
        return copy(ref, ref, pt_send, pt_recv, j, {"rows": partner})

    def taken(j):
        ref = cols.at[1 - core, rows_of(j)]
        return copy(ref, ref, pt_send, pt_recv, j, {"rows": partner})

    def send(make, j):
        @pl.when(j >= SLOTS)
        def _():
            make(j - SLOTS).wait_send()

        make(j).start()

    def line(held, make, j, first, last):
        @pl.when((j >= 0) & (j < count))
        def _():
            at, slot = rows_of(j), slot_of(j)

            @pl.when(first)
            def _():
                held[slot, :] = own[at, :]

            @pl.when(jnp.logical_not(first))
            def _():
                make(j).wait_recv()
                held[slot, :] = held[slot, :] + own[at, :]

            @pl.when(jnp.logical_not(last))
            def _():
                send(make, j)

    settle = HOP * jnp.maximum(l, loops - 1 - l)

    def multiply(g, n):
        at = pl.ds(pl.multiple_of(g * span, span), span)

        @pl.when(n == 0)
        def _():
            @pl.loop(0, mrows // 256)
            def _(m):
                mine = pl.ds(pl.multiple_of(m * 256, 256), 256)
                high, low = split(own[at, mine].T)
                left[mine, pl.ds(0, span)] = high
                left[mine, pl.ds(span, span)] = high
                left[mine, pl.ds(2 * span, span)] = low

        @pl.when(n < 2 * (mrows // 256))
        def _():
            block = n // (mrows // 256)
            inner = pl.multiple_of(lax.rem(n, mrows // 256) * 256, 256)
            high, low = split(cols[block, at, pl.ds(inner, 256)])
            right = jnp.concatenate([high, low, high], axis=0)
            theirs = pl.ds(pl.multiple_of(n * 256, 256), 256)

            @pl.loop(0, mrows // 256)
            def _(m):
                mine = pl.ds(pl.multiple_of(m * 256, 256), 256)
                part = jnp.dot(left[mine, :], right, preferred_element_type=jnp.float32) * scale

                @pl.when(g == 0)
                def _():
                    out_ref[mine, theirs] = part

                @pl.when(g > 0)
                def _():
                    out_ref[mine, theirs] = out_ref[mine, theirs] + part

    def step(t, carry):
        line(pin, up, t - HOP * l, l == 0, l == loops - 1)
        line(sin, down, t - HOP * (loops - 1 - l), l == loops - 1, l == 0)

        done = t - settle

        @pl.when((done >= 0) & (done < count))
        def _():
            at, slot = rows_of(done), slot_of(done)
            total = pin[slot, :] + (sin[slot, :] - own[at, :])
            own[at, :] = total

            @pl.when(far == 0)
            def _():
                cols[core, at, :] = total

        passed = done - REACH * far

        @pl.when((passed >= 0) & (passed < count))
        def _():
            @pl.when(far > 0)
            def _():
                chain(passed).wait_recv()

            @pl.when(far < pairs - 1)
            def _():
                send(chain, passed)

            send(share, passed)

        ready = done - REACH * pairs

        @pl.when((ready >= 0) & (ready < count))
        def _():
            taken(ready).wait_recv()

        @pl.when((ready >= GROUP) & (ready < count + GROUP))
        def _():
            multiply(ready // GROUP - 1, lax.rem(ready, GROUP))

        later = tiles + t // pace

        @pl.when((lax.rem(t, pace) == pace // 2) & (later < tile_count))
        def _():
            half(later)

        return carry

    lax.fori_loop(0, count + HOP * (loops - 1) + REACH * pairs + GROUP, step, 0)

    def drain(i, carry):
        j = count - SLOTS + i

        @pl.when(l < loops - 1)
        def _():
            up(j).wait_send()

        @pl.when(l > 0)
        def _():
            down(j).wait_send()

        @pl.when(far < pairs - 1)
        def _():
            chain(j).wait_send()

        share(j).wait_send()
        return carry

    lax.fori_loop(0, SLOTS, drain, 0)


def local(loops, row_count, integrals, mask, coeffs):
    nslab, naux, mrows, lcols = integrals.shape
    norbit = coeffs.shape[1]
    depth = nslab * naux * norbit
    count = depth // CHUNK
    wide = 2 * TILE
    assert lcols == 2 * mrows and row_count == 2 * loops and norbit % CHUNK == 0
    assert depth % (CHUNK * GROUP) == 0 and 2 * mrows // 256 <= GROUP
    ring = min(count, SLOTS + 3 * HOP * loops)
    spare = (8, 128) if lcols <= depth and norbit <= mrows else (lcols, norbit)
    blocks = jnp.repeat(mask.astype(jnp.float32), TILE, axis=2)
    blocks = blocks.reshape(nslab, mrows // wide, wide // TILE, lcols)
    dma = pltpu.SemaphoreType.DMA
    return pl.pallas_call(
        functools.partial(exchange_kernel, loops, row_count, float(depth) ** -0.5),
        out_shape=jax.ShapeDtypeStruct((mrows, lcols), jnp.float32),
        in_specs=[
            pl.BlockSpec(memory_space=pl.ANY),
            pl.BlockSpec(memory_space=pltpu.VMEM),
            pl.BlockSpec(memory_space=pl.ANY),
        ],
        out_specs=pl.BlockSpec(memory_space=pltpu.VMEM),
        scratch_shapes=[
            pltpu.VMEM((depth, mrows), jnp.float32),
            pltpu.VMEM((ring * CHUNK, mrows), jnp.float32),
            pltpu.VMEM((ring * CHUNK, mrows), jnp.float32),
            pltpu.VMEM((2, depth, mrows), jnp.float32),
            pltpu.VMEM((mrows, 3 * CHUNK * GROUP), jnp.bfloat16),
            pltpu.VMEM((norbit, lcols), jnp.bfloat16),
            pltpu.VMEM((norbit, lcols), jnp.bfloat16),
            pltpu.VMEM((2, wide, lcols), jnp.float32),
            pltpu.VMEM(spare, jnp.float32),
            dma((2,)),
            dma,
        ]
        + [dma((SLOTS,)), dma((count,))] * 4,
        compiler_params=pltpu.CompilerParams(
            collective_id=0, has_side_effects=True, vmem_limit_bytes=67043328
        ),
        name="exchange",
    )(integrals, blocks, coeffs)


def solution(mesh):
    in_specs = (P(None, None, "rows", "loop"), P(None, "rows", "loop"), P("loop", None))
    out_specs = P("rows", "loop")
    body = functools.partial(local, mesh.shape["loop"], mesh.shape["rows"])
    return jax.shard_map(body, mesh=mesh, in_specs=in_specs, out_specs=out_specs, check_vma=False)
```

time: 399 us -> 301 us (0.75)
  Pallas kernels: 378 us -> 290 us
  other arithmetic: 6.62 us -> 0.7 us
  local copies, waits for them, and re-layouts: 14.5 us -> 8.71 us
    pallas_call x1, Pallas kernels: 337 us -> 290 us  [local(): pl.pallas_call(functools.partial(exchange_kernel, loops, row_count, float...]
    pallas_call x1 -> x0, Pallas kernels: 40.6 us -> none  [half_partial(): pl.pallas_call(half_kernel, grid=(nslab, naux, mrows // tm), out_shape=ja...]
    convert_element_type x2 -> x1, other arithmetic: 6.62 us -> 0.7 us  [local(): blocks = jnp.repeat(mask.astype(jnp.float32), TILE, axis=2)]
    unnamed x2 -> x1, local copies, waits for them, and re-layouts: 13.8 us -> 7.89 us
where the time goes in v2:
time: 301 us; the launch traced here: 300 us
  Pallas kernels  290 us (96%)
  local copies, waits for them, and re-layouts  8.71 us (3%)
    pallas_call x1, Pallas kernels, local(): pl.pallas_call(functools.partial(exchange_kernel, loops, row_count, float...  290 us
    unnamed x1, local copies, waits for them, and re-layouts  7.89 us

profile of v2, /device:TPU:5, one launch (start us, length us, event | category | flops | bytes accessed | tf_op | source)
XLA Modules:
  0.0 299.6 jit_solution(15905434814481334301)
XLA Ops:
  0.0 0.7 convert_element_type.3
  0.7 0.1 broadcast_in_dim.3
  0.8 0.7 reshape_reshape.3.mask_ref
  1.5 290.2 %exchange.1 = f32[1024,2048]{1,0:T(8,128)} custom-call(f32[2,2,1024,2048]{3,2,1,0:T(8,128)} %integrals_ref.1, f32[2,4,2,2048]{3,2,1,0:T(2,128)} %reshape_reshape.3.mask_ref, f32[2048,640]{1,0:T(8,128)} %coeffs_ref.1), custom_call_target="tpu_custom_call" | custom-call | tf_op jit(solution)/shard_map/exchange/pallas_call | solution.py:293
  291.7 7.9 %copy.5 = f32[1024,2048]{1,0:T(8,128)} copy(f32[1024,2048]{1,0:T(8,128)} %exchange.1) | data formatting | bytes 16777216

commit v3 on v2

--- a/solution.py
+++ b/solution.py
@@ -8,11 +8,11 @@
 from jax.sharding import PartitionSpec as P
 
 TILE = 128
-CHUNK = 32
-GROUP = 8
-HOP = 2
+CHUNK = 16
+GROUP = 16
+HOP = 3
 REACH = 2
-SLOTS = 8
+SLOTS = 16
 MESH = pl.DeviceIdType.MESH
 
 

time: 301 us -> 330 us (1.096)
  Pallas kernels: 290 us -> 320 us
    pallas_call x1, Pallas kernels: 290 us -> 320 us  [local(): pl.pallas_call(functools.partial(exchange_kernel, loops, row_count, float...]
where the time goes in v3:
time: 330 us
  Pallas kernels  320 us (97%)
  local copies, waits for them, and re-layouts  8.71 us (3%)
    pallas_call x1, Pallas kernels, local(): pl.pallas_call(functools.partial(exchange_kernel, loops, row_count, float...  320 us
    unnamed x1, local copies, waits for them, and re-layouts  7.89 us

profile of v3, /device:TPU:5, one launch (start us, length us, event | category | flops | bytes accessed | tf_op | source)
XLA Modules:
  0.0 329.9 jit_solution(6562257954310427549)
XLA Ops:
  0.0 0.7 convert_element_type.3
  0.7 0.1 broadcast_in_dim.3
  0.8 0.7 reshape_reshape.3.mask_ref
  1.5 320.5 %exchange.1 = f32[1024,2048]{1,0:T(8,128)} custom-call(f32[2,2,1024,2048]{3,2,1,0:T(8,128)} %integrals_ref.1, f32[2,4,2,2048]{3,2,1,0:T(2,128)} %reshape_reshape.3.mask_ref, f32[2048,640]{1,0:T(8,128)} %coeffs_ref.1), custom_call_target="tpu_custom_call" | custom-call | tf_op jit(solution)/shard_map/exchange/pallas_call | solution.py:293
  322.0 7.9 %copy.5 = f32[1024,2048]{1,0:T(8,128)} copy(f32[1024,2048]{1,0:T(8,128)} %exchange.1) | data formatting | bytes 16777216

commit v4 on v2

--- a/solution.py
+++ b/solution.py
@@ -11,7 +11,7 @@
 CHUNK = 32
 GROUP = 8
 HOP = 2
-REACH = 2
+REACH = 1
 SLOTS = 8
 MESH = pl.DeviceIdType.MESH
 

time: 301 us -> 322 us (1.070)
  Pallas kernels: 290 us -> 313 us
    pallas_call x1, Pallas kernels: 290 us -> 313 us  [local(): pl.pallas_call(functools.partial(exchange_kernel, loops, row_count, float...]
where the time goes in v4:
time: 322 us
  Pallas kernels  313 us (97%)
  local copies, waits for them, and re-layouts  8.71 us (3%)
    pallas_call x1, Pallas kernels, local(): pl.pallas_call(functools.partial(exchange_kernel, loops, row_count, float...  313 us
    unnamed x1, local copies, waits for them, and re-layouts  7.89 us

profile of v4, /device:TPU:5, one launch (start us, length us, event | category | flops | bytes accessed | tf_op | source)
XLA Modules:
  0.0 322.2 jit_solution(12508055984081457824)
XLA Ops:
  0.0 0.7 convert_element_type.3
  0.7 0.1 broadcast_in_dim.3
  0.8 0.7 reshape_reshape.3.mask_ref
  1.5 312.8 %exchange.1 = f32[1024,2048]{1,0:T(8,128)} custom-call(f32[2,2,1024,2048]{3,2,1,0:T(8,128)} %integrals_ref.1, f32[2,4,2,2048]{3,2,1,0:T(2,128)} %reshape_reshape.3.mask_ref, f32[2048,640]{1,0:T(8,128)} %coeffs_ref.1), custom_call_target="tpu_custom_call" | custom-call | tf_op jit(solution)/shard_map/exchange/pallas_call | solution.py:293
  314.3 7.9 %copy.5 = f32[1024,2048]{1,0:T(8,128)} copy(f32[1024,2048]{1,0:T(8,128)} %exchange.1) | data formatting | bytes 16777216
